TPU v7x, 32 devices: a whole 2x2x4 slice. The times are simulated.
32 devices in a mesh: head: 4 (over z), span: 8 (over y, x, core).
Axes of the slice: x: 2, y: 2, z: 4, core: 2. Of those that a mesh axis runs over, the one named last changes fastest.
Arguments:
- queries: bfloat16 [4096, 2048], P(('span', 'head')), may hold values from -6 to 6
- keys: bfloat16 [4096, 2048], P(('span', 'head')), may hold values from -6 to 6
- values: bfloat16 [4096, 2048], P(('span', 'head')), may hold values from -6 to 6
- out_grad: bfloat16 [4096, 2048], P(('span', 'head')), may hold values from -6 to 6
Outputs:
- attn_out: bfloat16 [4096, 2048], P(('span', 'head'))
- query_gradient: bfloat16 [4096, 2048], P(('span', 'head'))
- grad_key: bfloat16 [4096, 2048], P(('span', 'head'))
- grad_value: bfloat16 [4096, 2048], P(('span', 'head'))
All inputs are finite; a program needn't handle non-finite values.
Results may differ from a plain program's by a relative error of at most 0.0058.
Values may be sent and summed in bfloat16 or wider, within the bound.
No kernel may reach another device: no remote copies, remote signals or barrier semaphores. Data moves between devices by JAX's collectives and lax.ppermute only.
A program may use at most 64 MiB of HBM per device.

v0:
```python
import jax
import jax.numpy as jnp
from jax import lax
from jax.sharding import PartitionSpec as P

HEADS = 16
DH = 128


def block_work(queries, keys, values, scaled, position_scale, forward_narrow, back_low):
    length = queries.shape[0]
    head_count = queries.shape[1]
    head_width = queries.shape[2]
    row_count = min(512, length)
    outputs = []
    query_grads = []
    key_acc = jnp.zeros((length, head_count, head_width), jnp.float32)
    value_acc = jnp.zeros((length, head_count, head_width), jnp.float32)
    for block_index in range(length // row_count):
        start_row = block_index * row_count
        end_row = start_row + row_count
        query_lines = queries[start_row:end_row]
        scaled_lines = scaled[start_row:end_row]
        key_cols = keys[:end_row]
        value_cols = values[:end_row]
        row_pos = start_row + lax.iota(jnp.int32, row_count)
        col_pos = lax.iota(jnp.int32, end_row)
        causal = col_pos[None, :] <= row_pos[:, None]
        raw_scores = jnp.einsum(
            "tnd,snd->nts", query_lines, key_cols, preferred_element_type=jnp.float32
        )
        scores = jnp.where(causal[None], raw_scores, 0.0).astype(jnp.bfloat16)
        raw_grads = jnp.einsum(
            "tnd,snd->nts", scaled_lines, value_cols, preferred_element_type=jnp.float32
        )
        score_gradient = jnp.where(causal[None], raw_grads, 0.0).astype(jnp.bfloat16)
        local_out = jnp.einsum(
            "epa,aev->pev", scores, value_cols, preferred_element_type=jnp.float32
        )
        carried_result = jnp.einsum(
            "rwb,wbo->rwo", query_lines, forward_narrow, preferred_element_type=jnp.float32
        )
        row_scale = position_scale[start_row:end_row]
        outputs.append(
            ((local_out + carried_result) * row_scale[:, None, None]).astype(jnp.bfloat16)
        )
        local_query = jnp.einsum(
            "epa,aev->pev", score_gradient, key_cols, preferred_element_type=jnp.float32
        )
        carried_query = jnp.einsum(
            "hsx,smx->hsm", scaled_lines, forward_narrow, preferred_element_type=jnp.float32
        )
        query_grads.append((local_query + carried_query).astype(jnp.bfloat16))
        key_acc = key_acc.at[:end_row].add(
            jnp.einsum(
                "nts,tnd->snd", score_gradient, query_lines, preferred_element_type=jnp.float32
            )
        )
        value_acc = value_acc.at[:end_row].add(
            jnp.einsum("nts,tnd->snd", scores, scaled_lines, preferred_element_type=jnp.float32)
        )
    grad_key = (
        key_acc + jnp.einsum("snv,nvk->snk", values, back_low, preferred_element_type=jnp.float32)
    ).astype(jnp.bfloat16)
    grad_value = (
        value_acc + jnp.einsum("snk,nvk->snv", keys, back_low, preferred_element_type=jnp.float32)
    ).astype(jnp.bfloat16)
    return (
        jnp.concatenate(outputs, axis=0),
        jnp.concatenate(query_grads, axis=0),
        grad_key,
        grad_value,
    )


def attend(pieces):
    queries = pieces[0][:, 0]
    keys = pieces[1][:, 0]
    values = pieces[2][:, 0]
    out_grad = pieces[3][:, 0]
    length = queries.shape[0]
    head_width = queries.shape[2]
    span_index = lax.axis_index("span")
    position = span_index * length + lax.iota(jnp.int32, length)
    position_scale = 1.0 / jnp.sqrt(jnp.float32(head_width) * (position + 1).astype(jnp.float32))
    scaled = (out_grad.astype(jnp.float32) * position_scale[:, None, None]).astype(jnp.bfloat16)
    forward_within = jnp.einsum("xgy,xgi->gyi", keys, values, preferred_element_type=jnp.float32)
    back_local = jnp.einsum("tnv,tnk->nvk", scaled, queries, preferred_element_type=jnp.float32)
    every_fwd, every_back = (
        lax.all_gather(forward_within[None], "span", axis=0, tiled=True),
        lax.all_gather(back_local[None], "span", axis=0, tiled=True),
    )
    block_order = lax.iota(jnp.int32, every_fwd.shape[0])
    lower_mask = (block_order < span_index).astype(jnp.float32)[:, None, None, None]
    upper_mask = (block_order > span_index).astype(jnp.float32)[:, None, None, None]
    fwd_state = jnp.sum(every_fwd * lower_mask, axis=0)
    back_state = jnp.sum(every_back * upper_mask, axis=0)
    forward_narrow = fwd_state.astype(jnp.bfloat16)
    back_low = back_state.astype(jnp.bfloat16)
    results = block_work(queries, keys, values, scaled, position_scale, forward_narrow, back_low)
    return (results[0][:, None], results[1][:, None], results[2][:, None], results[3][:, None])


def split_heads(matrix, group_count):
    return matrix.reshape(matrix.shape[0], group_count, HEADS // group_count, DH)


def merge_heads(grouped):
    return grouped.reshape(grouped.shape[0], HEADS * DH)


def shards(queries, keys, values, out_grad):
    group_count = lax.axis_size("head")
    results = attend(
        (
            lax.all_to_all(
                split_heads(queries, group_count), "head", split_axis=1, concat_axis=0, tiled=True
            ),
            lax.all_to_all(
                split_heads(keys, group_count), "head", split_axis=1, concat_axis=0, tiled=True
            ),
            lax.all_to_all(
                split_heads(values, group_count), "head", split_axis=1, concat_axis=0, tiled=True
            ),
            lax.all_to_all(
                split_heads(out_grad, group_count), "head", split_axis=1, concat_axis=0, tiled=True
            ),
        )
    )
    returned = (
        lax.all_to_all(results[0], "head", split_axis=0, concat_axis=1, tiled=True),
        lax.all_to_all(results[1], "head", split_axis=0, concat_axis=1, tiled=True),
        lax.all_to_all(results[2], "head", split_axis=0, concat_axis=1, tiled=True),
        lax.all_to_all(results[3], "head", split_axis=0, concat_axis=1, tiled=True),
    )
    return (
        merge_heads(returned[0]),
        merge_heads(returned[1]),
        merge_heads(returned[2]),
        merge_heads(returned[3]),
    )


def solution(mesh):
    return jax.shard_map(
        shards,
        mesh=mesh,
        in_specs=(
            P(("span", "head"), None),
            P(("span", "head"), None),
            P(("span", "head"), None),
            P(("span", "head"), None),
        ),
        out_specs=(
            P(("span", "head"), None),
            P(("span", "head"), None),
            P(("span", "head"), None),
            P(("span", "head"), None),
        ),
        check_vma=False,
    )
```

profile of v0, /device:TPU:0, one launch (start us, length us, event | category | flops | bytes accessed | tf_op | source)
XLA Modules:
  0.0 181.5 jit_solution(9970101980685170848)
XLA Ops:
  7.2 1.4 copy.49
  8.5 1.0 copy.50
  9.6 6.3 %all-to-all-start.1 = ((bf16[128,4,4,128]{3,0,2,1:T(8,128)(2,1)}), bf16[128,4,4,128]{3,0,2,1:T(8,128)(2,1)S(1)}, u32[]{:S(2)}, u32[]{:S(2)}) async-start(bf16[128,4,4,128]{3,0,2,1:T(8,128)(2,1)} %copy.50), calls=%async_computation.1 | async-start | bytes 1048576 | tf_op jit(solution)/shard_map/all_to_all | solution.py:119
  16.2 1.0 copy.53
  17.2 13.2 %all-to-all-done.1 = bf16[128,4,4,128]{3,0,2,1:T(8,128)(2,1)S(1)} async-done(((bf16[128,4,4,128]{3,0,2,1:T(8,128)(2,1)}), bf16[128,4,4,128]{3,0,2,1:T(8,128)(2,1)S(1)}, u32[]{:S(2)}, u32[]{:S(2)}) %all-to-all-start.1) | async-done | bytes 524320 | tf_op jit(solution)/shard_map/all_to_all | solution.py:119
  30.4 3.5 %all-to-all-start.2 = ((bf16[128,4,4,128]{3,0,2,1:T(8,128)(2,1)}), bf16[128,4,4,128]{3,0,2,1:T(8,128)(2,1)S(1)}, u32[]{:S(2)}, u32[]{:S(2)}) async-start(bf16[128,4,4,128]{3,0,2,1:T(8,128)(2,1)} %copy.53), calls=%async_computation.2 | async-start | bytes 1048576 | tf_op jit(solution)/shard_map/all_to_all | solution.py:122
  34.0 13.9 %all-to-all-done.2 = bf16[128,4,4,128]{3,0,2,1:T(8,128)(2,1)S(1)} async-done(((bf16[128,4,4,128]{3,0,2,1:T(8,128)(2,1)}), bf16[128,4,4,128]{3,0,2,1:T(8,128)(2,1)S(1)}, u32[]{:S(2)}, u32[]{:S(2)}) %all-to-all-start.2) | async-done | bytes 524320 | tf_op jit(solution)/shard_map/all_to_all | solution.py:122
  48.0 1.0 fusion.16
  49.3 1.0 copy.47
  50.3 3.5 %all-to-all-start = ((bf16[128,4,4,128]{3,0,2,1:T(8,128)(2,1)}), bf16[128,4,4,128]{3,0,2,1:T(8,128)(2,1)S(1)}, u32[]{:S(2)}, u32[]{:S(2)}) async-start(bf16[128,4,4,128]{3,0,2,1:T(8,128)(2,1)} %copy.47), calls=%async_computation | async-start | bytes 1048576 | tf_op jit(solution)/shard_map/all_to_all | solution.py:116
  54.1 1.0 copy.61
  55.1 12.7 %all-to-all-done = bf16[128,4,4,128]{3,0,2,1:T(8,128)(2,1)S(1)} async-done(((bf16[128,4,4,128]{3,0,2,1:T(8,128)(2,1)}), bf16[128,4,4,128]{3,0,2,1:T(8,128)(2,1)S(1)}, u32[]{:S(2)}, u32[]{:S(2)}) %all-to-all-start) | async-done | bytes 524320 | tf_op jit(solution)/shard_map/all_to_all | solution.py:116
  67.8 3.5 %all-to-all-start.4 = ((bf16[128,4,4,128]{3,0,2,1:T(8,128)(2,1)}), bf16[128,4,4,128]{3,0,2,1:T(8,128)(2,1)S(1)}, u32[]{:S(2)}, u32[]{:S(2)}) async-start(bf16[128,4,4,128]{3,0,2,1:T(8,128)(2,1)} %copy.61), calls=%async_computation.4 | async-start | bytes 1048576 | tf_op jit(solution)/shard_map/all_to_all | solution.py:125
  71.4 13.9 %all-to-all-done.4 = bf16[128,4,4,128]{3,0,2,1:T(8,128)(2,1)S(1)} async-done(((bf16[128,4,4,128]{3,0,2,1:T(8,128)(2,1)}), bf16[128,4,4,128]{3,0,2,1:T(8,128)(2,1)S(1)}, u32[]{:S(2)}, u32[]{:S(2)}) %all-to-all-start.4) | async-done | bytes 524320 | tf_op jit(solution)/shard_map/all_to_all | solution.py:125
  85.7 0.8 copy-done
  86.5 1.0 fusion.17
  87.6 0.7 copy-done.10
  88.3 1.8 %select_convert_fusion = bf16[4,512,512]{2,1,0:T(8,128)(2,1)S(1)} fusion(bf16[512,4,128]{2,0,1:T(8,128)(2,1)} %copy-done, bf16[512,4,128]{2,0,1:T(8,128)(2,1)S(1)} %bitcast.115, pred[512,512]{1,0:T(8,128)(4,1)S(1)} %iota_compare_fusion), kind=kOutput, calls=%fused_computation | convolution fusion | flops 270532608 | bytes 3407872 | tf_op jit(solution)/shard_map/tnd,snd->nts/dot_general | solution.py:33
  90.2 1.7 convolution_bitcast_fusion.1
  91.9 2.0 %multiply_reduce_fusion.1 = bf16[4,128,128]{2,1,0:T(8,128)(2,1)S(1)} fusion(f32[8,4,128,128]{3,2,1,0:T(8,128)} %bitcast.123, f32[8]{0:T(128)S(1)} %compare_convert_fusion.1), kind=kLoop, calls=%fused_computation.3 | loop fusion | flops 983040 | bytes 2228256 | tf_op jit(solution)/shard_map/reduce_sum | solution.py:96
  94.0 0.3 fusion.10
  94.3 1.2 copy.64
  95.5 4.1 %all-to-all-start.5 = ((bf16[512,1,4,128]{3,2,1,0:T(4,128)(2,1)}), bf16[512,1,4,128]{3,2,1,0:T(4,128)(2,1)}, u32[]{:S(2)}, u32[]{:S(2)}) async-start(bf16[512,1,4,128]{3,2,1,0:T(4,128)(2,1)} %copy.64), calls=%async_computation.5 | async-start | bytes 1048576 | tf_op jit(solution)/shard_map/all_to_all | solution.py:132
  99.7 2.9 %convolution_bitcast_fusion = f32[512,4,128]{2,0,1:T(8,128)} fusion(bf16[4,512,512]{2,1,0:T(8,128)(2,1)S(1)} %select_convert_fusion, bf16[512,4,128]{2,0,1:T(8,128)(2,1)} %bitcast.119), kind=kOutput, calls=%fused_computation.4 | convolution fusion | flops 268435456 | bytes 3670016 | tf_op jit(solution)/shard_map/nts,tnd->snd/dot_general | solution.py:55
  102.6 12.0 %all-gather.7.cloned.1.call-done = f32[32,128,128]{2,1,0:T(8,128)} async-done(((f32[4,128,128]{2,1,0:T(8,128)}), f32[32,128,128]{2,1,0:T(8,128)}) %all-gather.7.cloned.1.call-update) | async-done | bytes 2097168 | tf_op jit(solution)/shard_map/all_gather | solution.py:91
  114.6 1.8 %multiply_reduce_fusion = bf16[4,128,128]{2,1,0:T(8,128)(2,1)S(1)} fusion(f32[8,4,128,128]{3,2,1,0:T(8,128)} %bitcast.124, f32[8]{0:T(128)S(1)} %compare_convert_fusion), kind=kLoop, calls=%fused_computation.2 | loop fusion | flops 983040 | bytes 2228256 | tf_op jit(solution)/shard_map/reduce_sum | solution.py:97
  116.7 1.2 copy.70
  117.9 4.6 %all-to-all-start.6 = ((bf16[512,1,4,128]{3,2,1,0:T(4,128)(2,1)}), bf16[512,1,4,128]{3,2,1,0:T(4,128)(2,1)}, u32[]{:S(2)}, u32[]{:S(2)}) async-start(bf16[512,1,4,128]{3,2,1,0:T(4,128)(2,1)} %copy.70), calls=%async_computation.6 | async-start | bytes 1048576 | tf_op jit(solution)/shard_map/all_to_all | solution.py:133
  122.5 1.9 %select_convert_fusion.1 = bf16[4,512,512]{2,1,0:T(8,128)(2,1)S(1)} fusion(bf16[512,4,128]{2,0,1:T(8,128)(2,1)} %bitcast.120, bf16[512,4,128]{2,0,1:T(8,128)(2,1)S(1)} %bitcast.112, pred[512,512]{1,0:T(8,128)(4,1)} %copy-done.10), kind=kOutput, calls=%fused_computation.1 | convolution fusion | flops 270532608 | bytes 3407872 | tf_op jit(solution)/shard_map/tnd,snd->nts/dot_general | solution.py:29
  124.4 0.7 convolution_bitcast_fusion.2
  125.1 0.3 copy-done.4
  125.4 0.3 fusion.11
  125.7 1.2 copy.58
  126.9 10.6 %all-to-all-done.6 = bf16[512,1,4,128]{3,2,1,0:T(4,128)(2,1)} async-done(((bf16[512,1,4,128]{3,2,1,0:T(4,128)(2,1)}), bf16[512,1,4,128]{3,2,1,0:T(4,128)(2,1)}, u32[]{:S(2)}, u32[]{:S(2)}) %all-to-all-start.6) | async-done | bytes 524320 | tf_op jit(solution)/shard_map/all_to_all | solution.py:133
  137.5 4.1 %all-to-all-start.3 = ((bf16[512,1,4,128]{3,2,1,0:T(4,128)(2,1)}), bf16[512,1,4,128]{3,2,1,0:T(4,128)(2,1)}, u32[]{:S(2)}, u32[]{:S(2)}) async-start(bf16[512,1,4,128]{3,2,1,0:T(4,128)(2,1)} %copy.58), calls=%async_computation.3 | async-start | bytes 1048576 | tf_op jit(solution)/shard_map/all_to_all | solution.py:131
  141.7 0.5 fusion.18
  142.2 0.3 fusion.9
  142.5 1.1 copy.73
  143.5 12.2 %all-to-all-done.3 = bf16[512,1,4,128]{3,2,1,0:T(4,128)(2,1)} async-done(((bf16[512,1,4,128]{3,2,1,0:T(4,128)(2,1)}), bf16[512,1,4,128]{3,2,1,0:T(4,128)(2,1)}, u32[]{:S(2)}, u32[]{:S(2)}) %all-to-all-start.3) | async-done | bytes 524320 | tf_op jit(solution)/shard_map/all_to_all | solution.py:131
  155.8 3.6 %all-to-all-start.7 = ((bf16[512,1,4,128]{3,2,1,0:T(4,128)(2,1)}), bf16[512,1,4,128]{3,2,1,0:T(4,128)(2,1)S(1)}, u32[]{:S(2)}, u32[]{:S(2)}) async-start(bf16[512,1,4,128]{3,2,1,0:T(4,128)(2,1)} %copy.73), calls=%async_computation.7 | async-start | bytes 1048576 | tf_op jit(solution)/shard_map/all_to_all | solution.py:134
  159.4 1.2 copy.65
  160.7 1.2 reshape.143
  161.8 1.2 copy.71
  163.1 1.2 reshape.144
  164.2 1.2 copy.59
  165.5 1.2 reshape.141
  166.6 6.6 %all-to-all-done.7 = bf16[512,1,4,128]{3,2,1,0:T(4,128)(2,1)S(1)} async-done(((bf16[512,1,4,128]{3,2,1,0:T(4,128)(2,1)}), bf16[512,1,4,128]{3,2,1,0:T(4,128)(2,1)S(1)}, u32[]{:S(2)}, u32[]{:S(2)}) %all-to-all-start.7) | async-done | bytes 524320 | tf_op jit(solution)/shard_map/all_to_all | solution.py:134
  173.4 1.2 reshape.145
  (40 shorter events, 2.1 us)
Async XLA Ops:
  7.2 8.7 %copy-start.7 = (bf16[128,2048]{1,0:T(8,128)(2,1)S(1)}, bf16[128,2048]{1,0:T(8,128)(2,1)}, u32[]{:S(2)}) copy-start(bf16[128,2048]{1,0:T(8,128)(2,1)} %param.14) | copy-start | bytes 1572868
  9.6 20.8 %all-to-all-start.1 = ((bf16[128,4,4,128]{3,0,2,1:T(8,128)(2,1)}), bf16[128,4,4,128]{3,0,2,1:T(8,128)(2,1)S(1)}, u32[]{:S(2)}, u32[]{:S(2)}) async-start(bf16[128,4,4,128]{3,0,2,1:T(8,128)(2,1)} %copy.50), calls=%async_computation.1 | async-start | bytes 1048576 | tf_op jit(solution)/shard_map/all_to_all | solution.py:119
  30.4 17.5 %all-to-all-start.2 = ((bf16[128,4,4,128]{3,0,2,1:T(8,128)(2,1)}), bf16[128,4,4,128]{3,0,2,1:T(8,128)(2,1)S(1)}, u32[]{:S(2)}, u32[]{:S(2)}) async-start(bf16[128,4,4,128]{3,0,2,1:T(8,128)(2,1)} %copy.53), calls=%async_computation.2 | async-start | bytes 1048576 | tf_op jit(solution)/shard_map/all_to_all | solution.py:122
  33.9 15.2 %copy-start.8 = (bf16[128,2048]{1,0:T(8,128)(2,1)S(1)}, bf16[128,2048]{1,0:T(8,128)(2,1)}, u32[]{:S(2)}) copy-start(bf16[128,2048]{1,0:T(8,128)(2,1)} %param.12) | copy-start | bytes 1572868
  33.9 58.0 %all-gather.5.cloned.1.call-start = ((), (), s32[]{:S(2)}) async-start(), calls=%async_computation.8 | async-start | bytes 2359296 | tf_op jit(solution)/shard_map/all_gather | solution.py:90
  47.9 5.9 %copy-start.9 = (bf16[128,2048]{1,0:T(8,128)(2,1)S(1)}, bf16[128,2048]{1,0:T(8,128)(2,1)}, u32[]{:S(2)}) copy-start(bf16[128,2048]{1,0:T(8,128)(2,1)} %param.15) | copy-start | bytes 1572868
  50.3 17.5 %all-to-all-start = ((bf16[128,4,4,128]{3,0,2,1:T(8,128)(2,1)}), bf16[128,4,4,128]{3,0,2,1:T(8,128)(2,1)S(1)}, u32[]{:S(2)}, u32[]{:S(2)}) async-start(bf16[128,4,4,128]{3,0,2,1:T(8,128)(2,1)} %copy.47), calls=%async_computation | async-start | bytes 1048576 | tf_op jit(solution)/shard_map/all_to_all | solution.py:116
  67.8 17.5 %all-to-all-start.4 = ((bf16[128,4,4,128]{3,0,2,1:T(8,128)(2,1)}), bf16[128,4,4,128]{3,0,2,1:T(8,128)(2,1)S(1)}, u32[]{:S(2)}, u32[]{:S(2)}) async-start(bf16[128,4,4,128]{3,0,2,1:T(8,128)(2,1)} %copy.61), calls=%async_computation.4 | async-start | bytes 1048576 | tf_op jit(solution)/shard_map/all_to_all | solution.py:125
  71.3 43.3 %all-gather.7.cloned.1.call-start = ((), (), s32[]{:S(2)}) async-start(), calls=%async_computation.9 | async-start | bytes 2359296 | tf_op jit(solution)/shard_map/all_gather | solution.py:91
  71.4 14.3 %copy-start.3 = (bf16[4,128,1,4,128]{4,1,0,3,2:T(8,128)(2,1)}, bf16[4,128,1,4,128]{4,1,0,3,2:T(8,128)(2,1)S(1)}, u32[]{:S(2)}) copy-start(bf16[4,128,1,4,128]{4,1,0,3,2:T(8,128)(2,1)S(1)} %copy.48) | copy-start | bytes 1572868
  85.7 0.8 copy-start
  87.6 0.7 copy-start.10
  91.9 2.0 %copy-start.1 = (bf16[512,4,128]{2,0,1:T(8,128)(2,1)S(1)}, bf16[512,4,128]{2,0,1:T(8,128)(2,1)}, u32[]{:S(2)}) copy-start(bf16[512,4,128]{2,0,1:T(8,128)(2,1)} %copy-done) | copy-start | bytes 1572868
  91.9 2.1 %copy-start.6 = (f32[512,4,128]{2,0,1:T(8,128)S(1)}, f32[512,4,128]{2,0,1:T(8,128)}, u32[]{:S(2)}) copy-start(f32[512,4,128]{2,0,1:T(8,128)} %convolution_bitcast_fusion.1) | copy-start | bytes 3145732
  95.5 22.4 %all-to-all-start.5 = ((bf16[512,1,4,128]{3,2,1,0:T(4,128)(2,1)}), bf16[512,1,4,128]{3,2,1,0:T(4,128)(2,1)}, u32[]{:S(2)}, u32[]{:S(2)}) async-start(bf16[512,1,4,128]{3,2,1,0:T(4,128)(2,1)} %copy.64), calls=%async_computation.5 | async-start | bytes 1048576 | tf_op jit(solution)/shard_map/all_to_all | solution.py:132
  102.6 13.8 %copy-start.5 = (f32[512,4,128]{2,0,1:T(8,128)S(1)}, f32[512,4,128]{2,0,1:T(8,128)}, u32[]{:S(2)}) copy-start(f32[512,4,128]{2,0,1:T(8,128)} %convolution_bitcast_fusion) | copy-start | bytes 3145732
  117.9 19.6 %all-to-all-start.6 = ((bf16[512,1,4,128]{3,2,1,0:T(4,128)(2,1)}), bf16[512,1,4,128]{3,2,1,0:T(4,128)(2,1)}, u32[]{:S(2)}, u32[]{:S(2)}) async-start(bf16[512,1,4,128]{3,2,1,0:T(4,128)(2,1)} %copy.70), calls=%async_computation.6 | async-start | bytes 1048576 | tf_op jit(solution)/shard_map/all_to_all | solution.py:133
  124.4 1.0 copy-start.4
  125.4 16.2 %copy-start.2 = (bf16[512,4,128]{2,0,1:T(8,128)(2,1)S(1)}, bf16[512,4,128]{2,0,1:T(8,128)(2,1)}, u32[]{:S(2)}) copy-start(bf16[512,4,128]{2,0,1:T(8,128)(2,1)} %copy-done) | copy-start | bytes 1572868
  137.5 18.3 %all-to-all-start.3 = ((bf16[512,1,4,128]{3,2,1,0:T(4,128)(2,1)}), bf16[512,1,4,128]{3,2,1,0:T(4,128)(2,1)}, u32[]{:S(2)}, u32[]{:S(2)}) async-start(bf16[512,1,4,128]{3,2,1,0:T(4,128)(2,1)} %copy.58), calls=%async_computation.3 | async-start | bytes 1048576 | tf_op jit(solution)/shard_map/all_to_all | solution.py:131
  155.8 17.5 %all-to-all-start.7 = ((bf16[512,1,4,128]{3,2,1,0:T(4,128)(2,1)}), bf16[512,1,4,128]{3,2,1,0:T(4,128)(2,1)S(1)}, u32[]{:S(2)}, u32[]{:S(2)}) async-start(bf16[512,1,4,128]{3,2,1,0:T(4,128)(2,1)} %copy.73), calls=%async_computation.7 | async-start | bytes 1048576 | tf_op jit(solution)/shard_map/all_to_all | solution.py:134
Sparse Core Ops, SparseCore 0:
  49.2 26.8 all-gather.4
  87.7 26.8 all-gather.6
where the time goes:
time: 182 us; the launch traced here: 181 us
  waiting for transfers between devices  95.1 us (52%)
  starting transfers between devices  33.4 us (18%)
  local copies, waits for them, and re-layouts  21.6 us (12%)
  between operations  14.4 us (8%)
  matrix products  12.8 us (7%)
  other arithmetic  4.16 us (2%)
    all_to_all x1, waiting for transfers between devices, shards(): lax.all_to_all(split_heads(values, group_count), 'head', split_axis=1, co...  13.9 us
    all_to_all x1, waiting for transfers between devices, shards(): lax.all_to_all(split_heads(out_grad, group_count), 'head', split_axis=1,...  13.9 us
    all_to_all x1, waiting for transfers between devices, shards(): lax.all_to_all(split_heads(keys, group_count), 'head', split_axis=1, conc...  13.2 us
    all_to_all x1, waiting for transfers between devices, shards(): lax.all_to_all(split_heads(queries, group_count), 'head', split_axis=1, c...  12.7 us
    all_to_all x1, waiting for transfers between devices, shards(): lax.all_to_all(results[0], 'head', split_axis=0, concat_axis=1, tiled=True)  12.2 us
    all_gather x1, waiting for transfers between devices, attend(): lax.all_gather(back_local[None], 'span', axis=0, tiled=True)  12 us
    all_to_all x1, waiting for transfers between devices, shards(): lax.all_to_all(results[2], 'head', split_axis=0, concat_axis=1, tiled=True)  10.6 us
    all_to_all x1, waiting for transfers between devices, shards(): lax.all_to_all(results[3], 'head', split_axis=0, concat_axis=1, tiled=True)  6.61 us
  transfers between devices with their start and end apart: 10, of which 8 were waited for; matrix products, arithmetic and copies ran while one was open for 18% of the time, Pallas kernels for 0%

commit v1 on v0

--- a/solution.py
+++ b/solution.py
@@ -122,8 +122,16 @@
             lax.all_to_all(
                 split_heads(values, group_count), "head", split_axis=1, concat_axis=0, tiled=True
             ),
-            lax.all_to_all(
-                split_heads(out_grad, group_count), "head", split_axis=1, concat_axis=0, tiled=True
+            jnp.concatenate(
+                lax.all_to_all(
+                    jnp.stack(
+                        jnp.split(split_heads(out_grad, group_count), lax.axis_size("head"), axis=1)
+                    ),
+                    "head",
+                    0,
+                    0,
+                ),
+                axis=0,
             ),
         )
     )

time: 182 us -> 182 us (level)
    reshape x4 -> x3, local copies, waits for them, and re-layouts: 4.05 us -> 3.04 us  [split_heads(): matrix.reshape(matrix.shape[0], group_count, HEADS // group_count, DH)]
where the time goes in v1:
time: 182 us; the launch traced here: 181 us
  waiting for transfers between devices  95 us (52%)
  starting transfers between devices  33.4 us (18%)
  local copies, waits for them, and re-layouts  21.7 us (12%)
  between operations  14.4 us (8%)
  matrix products  12.8 us (7%)
  other arithmetic  4.14 us (2%)
    all_to_all x1, waiting for transfers between devices, shards(): lax.all_to_all(split_heads(values, group_count), 'head', split_axis=1, co...  13.9 us
    all_to_all x1, waiting for transfers between devices, shards(): lax.all_to_all(jnp.stack(jnp.split(split_heads(out_grad, group_count), la...  13.9 us
    all_to_all x1, waiting for transfers between devices, shards(): lax.all_to_all(split_heads(keys, group_count), 'head', split_axis=1, conc...  13.2 us
    all_to_all x1, waiting for transfers between devices, shards(): lax.all_to_all(split_heads(queries, group_count), 'head', split_axis=1, c...  12.6 us
    all_to_all x1, waiting for transfers between devices, shards(): lax.all_to_all(results[0], 'head', split_axis=0, concat_axis=1, tiled=True)  12.2 us
    all_gather x1, waiting for transfers between devices, attend(): lax.all_gather(back_local[None], 'span', axis=0, tiled=True)  12 us
    all_to_all x1, waiting for transfers between devices, shards(): lax.all_to_all(results[2], 'head', split_axis=0, concat_axis=1, tiled=True)  10.6 us
    all_to_all x1, waiting for transfers between devices, shards(): lax.all_to_all(results[3], 'head', split_axis=0, concat_axis=1, tiled=True)  6.61 us
  transfers between devices with their start and end apart: 10, of which 8 were waited for; matrix products, arithmetic and copies ran while one was open for 18% of the time, Pallas kernels for 0%

profile of v1, /device:TPU:0, one launch (start us, length us, event | category | flops | bytes accessed | tf_op | source)
XLA Modules:
  0.0 181.4 jit_solution(4253772384939842019)
XLA Ops:
  7.2 1.4 copy.52
  8.5 1.0 copy.53
  9.6 6.3 %all-to-all-start.1 = ((bf16[128,4,4,128]{3,0,2,1:T(8,128)(2,1)}), bf16[128,4,4,128]{3,0,2,1:T(8,128)(2,1)S(1)}, u32[]{:S(2)}, u32[]{:S(2)}) async-start(bf16[128,4,4,128]{3,0,2,1:T(8,128)(2,1)} %copy.53), calls=%async_computation.1 | async-start | bytes 1048576 | tf_op jit(solution)/shard_map/all_to_all | solution.py:119
  16.2 1.0 copy.56
  17.2 13.2 %all-to-all-done.1 = bf16[128,4,4,128]{3,0,2,1:T(8,128)(2,1)S(1)} async-done(((bf16[128,4,4,128]{3,0,2,1:T(8,128)(2,1)}), bf16[128,4,4,128]{3,0,2,1:T(8,128)(2,1)S(1)}, u32[]{:S(2)}, u32[]{:S(2)}) %all-to-all-start.1) | async-done | bytes 524320 | tf_op jit(solution)/shard_map/all_to_all | solution.py:119
  30.4 3.5 %all-to-all-start.2 = ((bf16[128,4,4,128]{3,0,2,1:T(8,128)(2,1)}), bf16[128,4,4,128]{3,0,2,1:T(8,128)(2,1)S(1)}, u32[]{:S(2)}, u32[]{:S(2)}) async-start(bf16[128,4,4,128]{3,0,2,1:T(8,128)(2,1)} %copy.56), calls=%async_computation.2 | async-start | bytes 1048576 | tf_op jit(solution)/shard_map/all_to_all | solution.py:122
  34.0 13.9 %all-to-all-done.2 = bf16[128,4,4,128]{3,0,2,1:T(8,128)(2,1)S(1)} async-done(((bf16[128,4,4,128]{3,0,2,1:T(8,128)(2,1)}), bf16[128,4,4,128]{3,0,2,1:T(8,128)(2,1)S(1)}, u32[]{:S(2)}, u32[]{:S(2)}) %all-to-all-start.2) | async-done | bytes 524320 | tf_op jit(solution)/shard_map/all_to_all | solution.py:122
  47.9 1.0 fusion.16
  49.3 1.0 copy.50
  50.3 3.5 %all-to-all-start = ((bf16[128,4,4,128]{3,0,2,1:T(8,128)(2,1)}), bf16[128,4,4,128]{3,0,2,1:T(8,128)(2,1)S(1)}, u32[]{:S(2)}, u32[]{:S(2)}) async-start(bf16[128,4,4,128]{3,0,2,1:T(8,128)(2,1)} %copy.50), calls=%async_computation | async-start | bytes 1048576 | tf_op jit(solution)/shard_map/all_to_all | solution.py:116
  54.2 1.0 copy.64
  55.2 12.6 %all-to-all-done = bf16[128,4,4,128]{3,0,2,1:T(8,128)(2,1)S(1)} async-done(((bf16[128,4,4,128]{3,0,2,1:T(8,128)(2,1)}), bf16[128,4,4,128]{3,0,2,1:T(8,128)(2,1)S(1)}, u32[]{:S(2)}, u32[]{:S(2)}) %all-to-all-start) | async-done | bytes 524320 | tf_op jit(solution)/shard_map/all_to_all | solution.py:116
  67.8 3.5 %all-to-all-start.4 = ((bf16[4,128,1,4,128]{4,1,3,2,0:T(8,128)(2,1)}), bf16[4,128,1,4,128]{4,1,3,2,0:T(8,128)(2,1)S(1)}, u32[]{:S(2)}, u32[]{:S(2)}) async-start(bf16[4,128,1,4,128]{4,1,3,2,0:T(8,128)(2,1)} %copy.64), calls=%async_computation.4 | async-start | bytes 1048576 | tf_op jit(solution)/shard_map/all_to_all | solution.py:126
  71.4 13.9 %all-to-all-done.4 = bf16[4,128,1,4,128]{4,1,3,2,0:T(8,128)(2,1)S(1)} async-done(((bf16[4,128,1,4,128]{4,1,3,2,0:T(8,128)(2,1)}), bf16[4,128,1,4,128]{4,1,3,2,0:T(8,128)(2,1)S(1)}, u32[]{:S(2)}, u32[]{:S(2)}) %all-to-all-start.4) | async-done | bytes 524320 | tf_op jit(solution)/shard_map/all_to_all | solution.py:126
  85.6 0.8 copy-done
  86.4 1.0 fusion.17
  87.5 0.7 copy-done.10
  88.3 1.8 select_convert_fusion
  90.1 1.7 convolution_bitcast_fusion.1
  91.8 2.0 %multiply_reduce_fusion.1 = bf16[4,128,128]{2,1,0:T(8,128)(2,1)S(1)} fusion(f32[8,4,128,128]{3,2,1,0:T(8,128)} %bitcast.126, f32[8]{0:T(128)S(1)} %compare_convert_fusion.1), kind=kLoop, calls=%fused_computation.3 | loop fusion | flops 983040 | bytes 2228256 | tf_op jit(solution)/shard_map/reduce_sum | solution.py:96
  93.9 0.3 fusion.10
  94.2 1.2 copy.67
  95.4 4.1 %all-to-all-start.5 = ((bf16[512,1,4,128]{3,2,1,0:T(4,128)(2,1)}), bf16[512,1,4,128]{3,2,1,0:T(4,128)(2,1)}, u32[]{:S(2)}, u32[]{:S(2)}) async-start(bf16[512,1,4,128]{3,2,1,0:T(4,128)(2,1)} %copy.67), calls=%async_computation.5 | async-start | bytes 1048576 | tf_op jit(solution)/shard_map/all_to_all | solution.py:140
  99.6 2.9 %convolution_bitcast_fusion = f32[512,4,128]{2,0,1:T(8,128)} fusion(bf16[4,512,512]{2,1,0:T(8,128)(2,1)S(1)} %select_convert_fusion, bf16[512,4,128]{2,0,1:T(8,128)(2,1)} %bitcast.122), kind=kOutput, calls=%fused_computation.4 | convolution fusion | flops 268435456 | bytes 3670016 | tf_op jit(solution)/shard_map/nts,tnd->snd/dot_general | solution.py:55
  102.5 12.0 %all-gather.7.cloned.1.call-done = f32[32,128,128]{2,1,0:T(8,128)} async-done(((f32[4,128,128]{2,1,0:T(8,128)}), f32[32,128,128]{2,1,0:T(8,128)}) %all-gather.7.cloned.1.call-update) | async-done | bytes 2097168 | tf_op jit(solution)/shard_map/all_gather | solution.py:91
  114.5 1.8 %multiply_reduce_fusion = bf16[4,128,128]{2,1,0:T(8,128)(2,1)S(1)} fusion(f32[8,4,128,128]{3,2,1,0:T(8,128)} %bitcast.127, f32[8]{0:T(128)S(1)} %compare_convert_fusion), kind=kLoop, calls=%fused_computation.2 | loop fusion | flops 983040 | bytes 2228256 | tf_op jit(solution)/shard_map/reduce_sum | solution.py:97
  116.6 1.2 copy.73
  117.8 4.6 %all-to-all-start.6 = ((bf16[512,1,4,128]{3,2,1,0:T(4,128)(2,1)}), bf16[512,1,4,128]{3,2,1,0:T(4,128)(2,1)}, u32[]{:S(2)}, u32[]{:S(2)}) async-start(bf16[512,1,4,128]{3,2,1,0:T(4,128)(2,1)} %copy.73), calls=%async_computation.6 | async-start | bytes 1048576 | tf_op jit(solution)/shard_map/all_to_all | solution.py:141
  122.4 1.9 %select_convert_fusion.1 = bf16[4,512,512]{2,1,0:T(8,128)(2,1)S(1)} fusion(bf16[512,4,128]{2,0,1:T(8,128)(2,1)} %bitcast.123, bf16[512,4,128]{2,0,1:T(8,128)(2,1)S(1)} %bitcast.115, pred[512,512]{1,0:T(8,128)(4,1)} %copy-done.10), kind=kOutput, calls=%fused_computation.1 | convolution fusion | flops 270532608 | bytes 3407872 | tf_op jit(solution)/shard_map/tnd,snd->nts/dot_general | solution.py:29
  124.3 0.7 convolution_bitcast_fusion.2
  125.0 0.3 copy-done.4
  125.3 0.3 fusion.11
  125.6 1.2 copy.61
  126.8 10.6 %all-to-all-done.6 = bf16[512,1,4,128]{3,2,1,0:T(4,128)(2,1)} async-done(((bf16[512,1,4,128]{3,2,1,0:T(4,128)(2,1)}), bf16[512,1,4,128]{3,2,1,0:T(4,128)(2,1)}, u32[]{:S(2)}, u32[]{:S(2)}) %all-to-all-start.6) | async-done | bytes 524320 | tf_op jit(solution)/shard_map/all_to_all | solution.py:141
  137.4 4.2 %all-to-all-start.3 = ((bf16[512,1,4,128]{3,2,1,0:T(4,128)(2,1)}), bf16[512,1,4,128]{3,2,1,0:T(4,128)(2,1)}, u32[]{:S(2)}, u32[]{:S(2)}) async-start(bf16[512,1,4,128]{3,2,1,0:T(4,128)(2,1)} %copy.61), calls=%async_computation.3 | async-start | bytes 1048576 | tf_op jit(solution)/shard_map/all_to_all | solution.py:139
  141.6 0.5 fusion.18
  142.1 0.3 fusion.9
  142.4 1.1 copy.76
  143.4 12.2 %all-to-all-done.3 = bf16[512,1,4,128]{3,2,1,0:T(4,128)(2,1)} async-done(((bf16[512,1,4,128]{3,2,1,0:T(4,128)(2,1)}), bf16[512,1,4,128]{3,2,1,0:T(4,128)(2,1)}, u32[]{:S(2)}, u32[]{:S(2)}) %all-to-all-start.3) | async-done | bytes 524320 | tf_op jit(solution)/shard_map/all_to_all | solution.py:139
  155.7 3.6 %all-to-all-start.7 = ((bf16[512,1,4,128]{3,2,1,0:T(4,128)(2,1)}), bf16[512,1,4,128]{3,2,1,0:T(4,128)(2,1)S(1)}, u32[]{:S(2)}, u32[]{:S(2)}) async-start(bf16[512,1,4,128]{3,2,1,0:T(4,128)(2,1)} %copy.76), calls=%async_computation.7 | async-start | bytes 1048576 | tf_op jit(solution)/shard_map/all_to_all | solution.py:142
  159.3 1.2 copy.68
  160.6 1.2 reshape.140
  161.7 1.2 copy.74
  163.0 1.2 reshape.141
  164.1 1.2 copy.62
  165.4 1.2 reshape.138
  166.5 6.6 %all-to-all-done.7 = bf16[512,1,4,128]{3,2,1,0:T(4,128)(2,1)S(1)} async-done(((bf16[512,1,4,128]{3,2,1,0:T(4,128)(2,1)}), bf16[512,1,4,128]{3,2,1,0:T(4,128)(2,1)S(1)}, u32[]{:S(2)}, u32[]{:S(2)}) %all-to-all-start.7) | async-done | bytes 524320 | tf_op jit(solution)/shard_map/all_to_all | solution.py:142
  173.3 1.2 reshape.142
  (41 shorter events, 2.1 us)
Async XLA Ops:
  7.2 8.7 %copy-start.7 = (bf16[128,2048]{1,0:T(8,128)(2,1)S(1)}, bf16[128,2048]{1,0:T(8,128)(2,1)}, u32[]{:S(2)}) copy-start(bf16[128,2048]{1,0:T(8,128)(2,1)} %param.14) | copy-start | bytes 1572868
  9.6 20.8 %all-to-all-start.1 = ((bf16[128,4,4,128]{3,0,2,1:T(8,128)(2,1)}), bf16[128,4,4,128]{3,0,2,1:T(8,128)(2,1)S(1)}, u32[]{:S(2)}, u32[]{:S(2)}) async-start(bf16[128,4,4,128]{3,0,2,1:T(8,128)(2,1)} %copy.53), calls=%async_computation.1 | async-start | bytes 1048576 | tf_op jit(solution)/shard_map/all_to_all | solution.py:119
  30.4 17.5 %all-to-all-start.2 = ((bf16[128,4,4,128]{3,0,2,1:T(8,128)(2,1)}), bf16[128,4,4,128]{3,0,2,1:T(8,128)(2,1)S(1)}, u32[]{:S(2)}, u32[]{:S(2)}) async-start(bf16[128,4,4,128]{3,0,2,1:T(8,128)(2,1)} %copy.56), calls=%async_computation.2 | async-start | bytes 1048576 | tf_op jit(solution)/shard_map/all_to_all | solution.py:122
  33.9 15.1 %copy-start.8 = (bf16[128,2048]{1,0:T(8,128)(2,1)S(1)}, bf16[128,2048]{1,0:T(8,128)(2,1)}, u32[]{:S(2)}) copy-start(bf16[128,2048]{1,0:T(8,128)(2,1)} %param.12) | copy-start | bytes 1572868
  33.9 57.9 %all-gather.5.cloned.1.call-start = ((), (), s32[]{:S(2)}) async-start(), calls=%async_computation.8 | async-start | bytes 2359296 | tf_op jit(solution)/shard_map/all_gather | solution.py:90
  47.9 5.9 %copy-start.9 = (bf16[128,2048]{1,0:T(8,128)(2,1)S(1)}, bf16[128,2048]{1,0:T(8,128)(2,1)}, u32[]{:S(2)}) copy-start(bf16[128,2048]{1,0:T(8,128)(2,1)} %param.15) | copy-start | bytes 1572868
  50.3 17.5 %all-to-all-start = ((bf16[128,4,4,128]{3,0,2,1:T(8,128)(2,1)}), bf16[128,4,4,128]{3,0,2,1:T(8,128)(2,1)S(1)}, u32[]{:S(2)}, u32[]{:S(2)}) async-start(bf16[128,4,4,128]{3,0,2,1:T(8,128)(2,1)} %copy.50), calls=%async_computation | async-start | bytes 1048576 | tf_op jit(solution)/shard_map/all_to_all | solution.py:116
  67.8 17.5 %all-to-all-start.4 = ((bf16[4,128,1,4,128]{4,1,3,2,0:T(8,128)(2,1)}), bf16[4,128,1,4,128]{4,1,3,2,0:T(8,128)(2,1)S(1)}, u32[]{:S(2)}, u32[]{:S(2)}) async-start(bf16[4,128,1,4,128]{4,1,3,2,0:T(8,128)(2,1)} %copy.64), calls=%async_computation.4 | async-start | bytes 1048576 | tf_op jit(solution)/shard_map/all_to_all | solution.py:126
  71.3 43.2 %all-gather.7.cloned.1.call-start = ((), (), s32[]{:S(2)}) async-start(), calls=%async_computation.9 | async-start | bytes 2359296 | tf_op jit(solution)/shard_map/all_gather | solution.py:91
  71.4 16.0 %copy-start.3 = (bf16[4,128,1,4,128]{4,1,0,3,2:T(8,128)(2,1)}, bf16[4,128,1,4,128]{4,1,0,3,2:T(8,128)(2,1)S(1)}, u32[]{:S(2)}) copy-start(bf16[4,128,1,4,128]{4,1,0,3,2:T(8,128)(2,1)S(1)} %copy.51) | copy-start | bytes 1572868
  85.6 0.8 copy-start
  87.5 0.7 copy-start.10
  91.8 2.0 %copy-start.1 = (bf16[512,4,128]{2,0,1:T(8,128)(2,1)S(1)}, bf16[512,4,128]{2,0,1:T(8,128)(2,1)}, u32[]{:S(2)}) copy-start(bf16[512,4,128]{2,0,1:T(8,128)(2,1)} %copy-done) | copy-start | bytes 1572868
  91.8 2.1 %copy-start.6 = (f32[512,4,128]{2,0,1:T(8,128)S(1)}, f32[512,4,128]{2,0,1:T(8,128)}, u32[]{:S(2)}) copy-start(f32[512,4,128]{2,0,1:T(8,128)} %convolution_bitcast_fusion.1) | copy-start | bytes 3145732
  95.4 22.4 %all-to-all-start.5 = ((bf16[512,1,4,128]{3,2,1,0:T(4,128)(2,1)}), bf16[512,1,4,128]{3,2,1,0:T(4,128)(2,1)}, u32[]{:S(2)}, u32[]{:S(2)}) async-start(bf16[512,1,4,128]{3,2,1,0:T(4,128)(2,1)} %copy.67), calls=%async_computation.5 | async-start | bytes 1048576 | tf_op jit(solution)/shard_map/all_to_all | solution.py:140
  102.5 13.8 %copy-start.5 = (f32[512,4,128]{2,0,1:T(8,128)S(1)}, f32[512,4,128]{2,0,1:T(8,128)}, u32[]{:S(2)}) copy-start(f32[512,4,128]{2,0,1:T(8,128)} %convolution_bitcast_fusion) | copy-start | bytes 3145732
  117.8 19.6 %all-to-all-start.6 = ((bf16[512,1,4,128]{3,2,1,0:T(4,128)(2,1)}), bf16[512,1,4,128]{3,2,1,0:T(4,128)(2,1)}, u32[]{:S(2)}, u32[]{:S(2)}) async-start(bf16[512,1,4,128]{3,2,1,0:T(4,128)(2,1)} %copy.73), calls=%async_computation.6 | async-start | bytes 1048576 | tf_op jit(solution)/shard_map/all_to_all | solution.py:141
  124.3 1.0 copy-start.4
  125.3 16.2 %copy-start.2 = (bf16[512,4,128]{2,0,1:T(8,128)(2,1)S(1)}, bf16[512,4,128]{2,0,1:T(8,128)(2,1)}, u32[]{:S(2)}) copy-start(bf16[512,4,128]{2,0,1:T(8,128)(2,1)} %copy-done) | copy-start | bytes 1572868
  137.4 18.3 %all-to-all-start.3 = ((bf16[512,1,4,128]{3,2,1,0:T(4,128)(2,1)}), bf16[512,1,4,128]{3,2,1,0:T(4,128)(2,1)}, u32[]{:S(2)}, u32[]{:S(2)}) async-start(bf16[512,1,4,128]{3,2,1,0:T(4,128)(2,1)} %copy.61), calls=%async_computation.3 | async-start | bytes 1048576 | tf_op jit(solution)/shard_map/all_to_all | solution.py:139
  155.7 17.5 %all-to-all-start.7 = ((bf16[512,1,4,128]{3,2,1,0:T(4,128)(2,1)}), bf16[512,1,4,128]{3,2,1,0:T(4,128)(2,1)S(1)}, u32[]{:S(2)}, u32[]{:S(2)}) async-start(bf16[512,1,4,128]{3,2,1,0:T(4,128)(2,1)} %copy.76), calls=%async_computation.7 | async-start | bytes 1048576 | tf_op jit(solution)/shard_map/all_to_all | solution.py:142
Sparse Core Ops, SparseCore 0:
  49.1 26.8 all-gather.4
  87.5 26.8 all-gather.6
